TPU v7x, 32 devices: a whole 2x2x4 slice. The times are simulated.
32 devices in a mesh: space: 16 (over z, y, x), mem: 2 (over core).
Axes of the slice: x: 2, y: 2, z: 4, core: 2. Of those that a mesh axis runs over, the one named last changes fastest.
Arguments:
- perturb: float32 [1024, 4096], P(('space', 'mem')), may hold values from -6 to 6
- pair_list: int32 [64, 3], P('space'), may hold values from 0 to 15, as said below
- pair_count: int32 [16], P('space'), may hold values from 1 to 4, as said below
- band_weight: float32 [8], replicated, may hold values from 0.25 to 1
- cov_scale: float32 [1], replicated, may hold values from 0.5 to 2
- target: float32 [4096, 1024], P('space', 'mem'), may hold values from -6 to 6
- first_guess: float32 [4096, 1024], P('space', 'mem'), may hold values from -6 to 6
Outputs:
- solution: float32 [4096, 1024], P('space', 'mem')
Inputs may be any that keep to these rules, and one draw needn't show every extreme that they name: `pair_list`: rows 4 * s to 4 * s + 3 are owner s's slots. The first block of each is owner s's own block s; the second is the first plus d modulo 16, with 0 <= d <= 3; each of the four pairs (d = 0 to 3) stands in exactly one slot of its owner. The third column is an index into band_weight. Only the first pair_count[s] slots of owner s are live; in every draw some owner has all 4 slots live.
All inputs are finite; a program needn't handle non-finite values.
Results may differ from a plain program's by a relative error of at most 0.0003.
Values sent between devices are 32-bit elements; how exact they have to be, the bound alone decides.
A program may use at most 64 MiB of HBM per device.

v0:
```python
import jax
import jax.numpy as jnp
from jax import lax
from jax.sharding import PartitionSpec as P

BLOCK = 256
MEMBERS = 1024
REACH_DEV = 3
NBANDS = 8
ITERS = 2


def shifted(array, axis, by):
    count = lax.axis_size(axis)
    return lax.ppermute(array, axis, [(i, (i + by) % count) for i in range(count)])


def fetch_members(own_members):
    pieces = [own_members]
    for offset in range(1, REACH_DEV + 1):
        pieces.append(shifted(own_members, "space", -offset))
    return jnp.concatenate(pieces, axis=1)


def fetch_field(iterate):
    pieces = [iterate]
    for offset in range(1, REACH_DEV + 1):
        pieces.append(shifted(iterate, "space", -offset))
    return jnp.concatenate(pieces, axis=0)


def return_partials(pieces):
    total = pieces[0]
    for offset in range(1, REACH_DEV + 1):
        total = total + shifted(pieces[offset], "space", offset)
    return total


def per_device(perturb, pair_list, pair_count, band_weight, cov_scale, target, first_guess):
    own_members = lax.all_to_all(perturb, "space", split_axis=1, concat_axis=0, tiled=True)
    rows_dev = own_members.shape[1]
    blocks_dev = rows_dev // BLOCK
    blocks_near = (REACH_DEV + 1) * blocks_dev
    blocks_all = blocks_dev * lax.axis_size("space")
    slot_total = pair_list.shape[0]
    first_local = (pair_list[:, 0] - lax.axis_index("space") * blocks_dev) % blocks_all
    second_local = (pair_list[:, 1] - lax.axis_index("space") * blocks_dev) % blocks_all
    living = (jnp.arange(slot_total, dtype=jnp.int32) < pair_count[0]).astype(jnp.float32)
    band_table = (pair_list[:, 2][:, None] == jnp.arange(NBANDS, dtype=jnp.int32)[None, :]).astype(
        jnp.float32
    )
    band_now = jnp.dot(
        band_table, band_weight, precision=lax.Precision.HIGHEST, preferred_element_type=jnp.float32
    )
    weights = cov_scale[0] * band_now * living / (MEMBERS - 1)
    members_near = fetch_members(own_members)

    def build_tile(slot_pair):
        first_cols = lax.dynamic_slice_in_dim(members_near, slot_pair[0] * BLOCK, BLOCK, 1)
        second_cols = lax.dynamic_slice_in_dim(members_near, slot_pair[1] * BLOCK, BLOCK, 1)
        return jnp.einsum(
            "ma,mb->ab",
            first_cols,
            second_cols,
            precision=lax.Precision.HIGHEST,
            preferred_element_type=jnp.float32,
        )

    partial_value = (
        lax.map(build_tile, jnp.stack([first_local, second_local], 1)) * weights[:, None, None]
    )
    tiles = lax.psum(partial_value, "mem")
    block_ids = jnp.arange(blocks_near, dtype=jnp.int32)
    first_select = (first_local[:, None] == block_ids[None, :]).astype(jnp.float32)
    second_select = (second_local[:, None] == block_ids[None, :]).astype(jnp.float32)
    mirror_mask = (first_local != second_local).astype(jnp.float32)
    iterate = first_guess
    columns = iterate.shape[1]
    for sweep in range(ITERS):
        field_near = fetch_field(iterate).reshape(blocks_near, BLOCK, columns)
        near_blocks = jnp.take(field_near, second_local, axis=0)
        own_blocks = jnp.take(field_near, first_local, axis=0)
        forward = jnp.einsum(
            "pab,pbc->pac",
            tiles,
            near_blocks,
            precision=lax.Precision.HIGHEST,
            preferred_element_type=jnp.float32,
        )
        mirror = jnp.einsum(
            "pab,pac->pbc",
            tiles,
            own_blocks,
            precision=lax.Precision.HIGHEST,
            preferred_element_type=jnp.float32,
        )
        mirror = mirror * mirror_mask[:, None, None]
        collected = jnp.einsum(
            "pl,pac->lac",
            first_select,
            forward,
            precision=lax.Precision.HIGHEST,
            preferred_element_type=jnp.float32,
        )
        collected = collected + jnp.einsum(
            "pl,pac->lac",
            second_select,
            mirror,
            precision=lax.Precision.HIGHEST,
            preferred_element_type=jnp.float32,
        )
        applied = return_partials([collected[offset] for offset in range(REACH_DEV + 1)])
        iterate = iterate + 0.5 * (target - iterate - applied)
    return iterate


def solution(mesh):
    in_specs = (
        P(("space", "mem"), None),
        P("space", None),
        P("space"),
        P(),
        P(),
        P("space", "mem"),
        P("space", "mem"),
    )
    out_specs = P("space", "mem")
    return jax.shard_map(
        per_device, mesh=mesh, in_specs=in_specs, out_specs=out_specs, check_vma=False
    )
```

profile of v0, /device:TPU:2, one launch (start us, length us, event | category | flops | bytes accessed | tf_op | source)
XLA Modules:
  0.0 288.0 jit_solution(15387314568821327748)
XLA Ops:
  6.5 1.9 copy.56
  8.5 7.3 %all-to-all-start = ((f32[32,16,256]{2,0,1:T(8,128)}), f32[32,16,256]{2,0,1:T(8,128)S(1)}, u32[]{:S(2)}, u32[]{:S(2)}) async-start(f32[32,16,256]{2,0,1:T(8,128)} %bitcast.87), calls=%async_computation | async-start | bytes 1048576 | tf_op jit(solution)/shard_map/all_to_all | solution.py:40
  15.9 4.2 %collective-permute-start.4 = (f32[256,512]{1,0:T(8,128)S(1)}, f32[256,512]{1,0:T(8,128)}, u32[]{:S(2)}, u32[]{:S(2)}) collective-permute-start(f32[256,512]{1,0:T(8,128)S(1)} %copy-done.8), channel_id=1, source_target_pairs={{0,28},{2,30},{4,0},{6,2},{8,4},{10,6},{12,8},{14,10},{16,12},{18,... | collective-permute-start | bytes 1572872 | tf_op jit(solution)/shard_map/ppermute | solution.py:15
  22.4 7.6 %all-to-all-done = f32[32,16,256]{2,0,1:T(8,128)S(1)} async-done(((f32[32,16,256]{2,0,1:T(8,128)}), f32[32,16,256]{2,0,1:T(8,128)S(1)}, u32[]{:S(2)}, u32[]{:S(2)}) %all-to-all-start) | async-done | bytes 524320 | tf_op jit(solution)/shard_map/all_to_all | solution.py:40
  29.9 23.3 %collective-permute-start.2 = (f32[512,256]{1,0:T(8,128)S(1)}, f32[512,256]{1,0:T(8,128)S(1)}, u32[]{:S(2)}, u32[]{:S(2)}) collective-permute-start(f32[512,256]{1,0:T(8,128)S(1)} %bitcast.103), channel_id=1, source_target_pairs={{0,26},{2,28},{4,30},{6,0},{8,2},{10,4},{12,6},{14,8},{16,10},{18,... | collective-permute-start | bytes 1572872 | tf_op jit(solution)/shard_map/ppermute | solution.py:15
  53.3 1.8 collective-permute-start.1
  55.0 1.3 collective-permute-start
  56.6 9.0 %collective-permute-done.2 = f32[512,256]{1,0:T(8,128)S(1)} collective-permute-done((f32[512,256]{1,0:T(8,128)S(1)}, f32[512,256]{1,0:T(8,128)S(1)}, u32[]{:S(2)}, u32[]{:S(2)}) %collective-permute-start.2) | collective-permute-done | bytes 524320 | tf_op jit(solution)/shard_map/ppermute | solution.py:15
  65.6 6.2 %collective-permute-start.5 = (f32[256,512]{1,0:T(8,128)S(1)}, f32[256,512]{1,0:T(8,128)}, u32[]{:S(2)}, u32[]{:S(2)}) collective-permute-start(f32[256,512]{1,0:T(8,128)S(1)} %copy-done.8), channel_id=1, source_target_pairs={{0,26},{2,28},{4,30},{6,0},{8,2},{10,4},{12,6},{14,8},{16,10},{18,... | collective-permute-start | bytes 1572872 | tf_op jit(solution)/shard_map/ppermute | solution.py:15
  71.8 4.9 %collective-permute-done.1 = f32[512,256]{1,0:T(8,128)S(1)} collective-permute-done((f32[512,256]{1,0:T(8,128)S(1)}, f32[512,256]{1,0:T(8,128)S(1)}, u32[]{:S(2)}, u32[]{:S(2)}) %collective-permute-start.1) | collective-permute-done | bytes 524320 | tf_op jit(solution)/shard_map/ppermute | solution.py:15
  76.7 3.1 %collective-permute-done = f32[512,256]{1,0:T(8,128)S(1)} collective-permute-done((f32[512,256]{1,0:T(8,128)S(1)}, f32[512,256]{1,0:T(8,128)S(1)}, u32[]{:S(2)}, u32[]{:S(2)}) %collective-permute-start) | collective-permute-done | bytes 524320 | tf_op jit(solution)/shard_map/ppermute | solution.py:15
  80.1 15.1 %while.10 = (s32[]{:T(128)}, f32[4,256,256]{2,1,0:T(8,128)}, s32[4,2]{0,1:T(2,128)S(1)}, f32[512,1024]{1,0:T(8,128)S(1)}, s32[]{:T(128)}, /*index=5*/s32[1,1]{0,1:T(1,128)}, s32[]{:T(128)}, s32[]{:T(128)}) while((s32[]{:T(128)}, f32[4,256,256]{2,1,0:T(8,128)}, s32[4,2]{0,1:T(2,128)S(1)}, f32[512,1024]{1,0:T(8,128)S(1)}, s32[]{:T(128)}, ...), condition=%wide.region_1.2_spmd, body=%wide.region_0.1_spmd.sunk | while | flops 402653184 | bytes 1310953 | solution.py:70
  82.2 1.7 fusion.79
  85.9 1.8 fusion.79
  89.7 1.8 fusion.79
  93.5 1.8 fusion.79
  95.2 2.4 broadcast_multiply_fusion
  97.7 3.7 %collective-permute-done.5 = f32[256,512]{1,0:T(8,128)} collective-permute-done((f32[256,512]{1,0:T(8,128)S(1)}, f32[256,512]{1,0:T(8,128)}, u32[]{:S(2)}, u32[]{:S(2)}) %collective-permute-start.5) | collective-permute-done | bytes 524320 | tf_op jit(solution)/shard_map/ppermute | solution.py:15
  101.4 1.6 pad_maximum_fusion.1
  103.0 2.0 gather_fusion.1
  105.0 2.0 gather_fusion
  107.1 26.6 %all-reduce.2.cloned.1.call-done = f32[4,256,256]{2,1,0:T(8,128)} async-done(((f32[4,256,256]{2,1,0:T(8,128)}), f32[4,256,256]{2,1,0:T(8,128)}) %all-reduce.2.cloned.1.call-update) | async-done | bytes 1048592 | tf_op jit(solution)/shard_map/psum | solution.py:72
  133.7 4.2 %fusion.14 = f32[4,256,512]{2,1,0:T(8,128)S(1)} fusion(f32[4,256,256]{2,1,0:T(8,128)} %all-reduce.2.cloned.1.call-done, f32[4,256,512]{2,1,0:T(8,128)} %gather_fusion.1, pred[4]{0:T(512)(128)(4,1)S(1)} %compare_and_fusion), kind=kOutput, calls=%fused_computation.26 | convolution fusion | flops 1611137024 | bytes 5242884 | tf_op jit(solution)/shard_map/pab,pac->pbc/dot_general | solution.py:90
  137.9 3.3 %fusion.7 = f32[4,256,512]{2,0,1:T(4,128)S(1)} fusion(f32[4,256,512]{2,1,0:T(8,128)S(1)} %fusion.14, f32[4]{0:T(128)S(1)} %get-tuple-element.39, s32[4]{0:T(128)S(1)} %bitcast.113), kind=kOutput, calls=%fused_computation.18 | convolution fusion | flops 25690128 | bytes 4194336 | tf_op jit(solution)/shard_map/pl,pac->lac/dot_general | solution.py:105
  141.3 2.1 fusion.16
  143.4 3.8 %fusion.18 = f32[4,256,512]{2,0,1:T(4,128)S(1)} fusion(f32[4,256,512]{2,0,1:T(4,128)S(1)} %fusion.7, f32[4,256,512]{2,1,0:T(8,128)S(1)} %fusion.16, s32[4]{0:T(128)S(1)} %bitcast.111), kind=kOutput, calls=%fused_computation.30 | convolution fusion | flops 25690128 | bytes 6291472 | tf_op jit(solution)/shard_map/pl,pac->lac/dot_general | solution.py:98
  147.2 1.5 fusion.67
  148.9 1.5 collective-permute-start.7
  150.4 1.5 collective-permute-start.8
  151.9 2.4 collective-permute-start.6
  154.2 19.0 %collective-permute-done.7 = f32[256,512]{1,0:T(8,128)S(1)} collective-permute-done((f32[256,512]{1,0:T(8,128)S(1)}, f32[256,512]{1,0:T(8,128)S(1)}, u32[]{:S(2)}, u32[]{:S(2)}) %collective-permute-start.7) | collective-permute-done | bytes 524320 | tf_op jit(solution)/shard_map/ppermute | solution.py:15
  173.3 3.7 %collective-permute-done.8 = f32[256,512]{1,0:T(8,128)S(1)} collective-permute-done((f32[256,512]{1,0:T(8,128)S(1)}, f32[256,512]{1,0:T(8,128)S(1)}, u32[]{:S(2)}, u32[]{:S(2)}) %collective-permute-start.8) | collective-permute-done | bytes 524320 | tf_op jit(solution)/shard_map/ppermute | solution.py:15
  177.3 3.7 %collective-permute-start.11 = (f32[256,512]{1,0:T(8,128)S(1)}, f32[256,512]{1,0:T(8,128)S(1)}, u32[]{:S(2)}, u32[]{:S(2)}) collective-permute-start(f32[256,512]{1,0:T(8,128)S(1)} %fusion.45), channel_id=1, source_target_pairs={{0,26},{2,28},{4,30},{6,0},{8,2},{10,4},{12,6},{14,8},{16,10},{18,... | collective-permute-start | bytes 1572872 | tf_op jit(solution)/shard_map/ppermute | solution.py:15
  181.0 11.5 %collective-permute-start.10 = (f32[256,512]{1,0:T(8,128)S(1)}, f32[256,512]{1,0:T(8,128)S(1)}, u32[]{:S(2)}, u32[]{:S(2)}) collective-permute-start(f32[256,512]{1,0:T(8,128)S(1)} %fusion.45), channel_id=1, source_target_pairs={{0,28},{2,30},{4,0},{6,2},{8,4},{10,6},{12,8},{14,10},{16,12},{18,... | collective-permute-start | bytes 1572872 | tf_op jit(solution)/shard_map/ppermute | solution.py:15
  192.5 9.5 %collective-permute-done.11 = f32[256,512]{1,0:T(8,128)S(1)} collective-permute-done((f32[256,512]{1,0:T(8,128)S(1)}, f32[256,512]{1,0:T(8,128)S(1)}, u32[]{:S(2)}, u32[]{:S(2)}) %collective-permute-start.11) | collective-permute-done | bytes 524320 | tf_op jit(solution)/shard_map/ppermute | solution.py:15
  202.0 12.0 %collective-permute-done.10 = f32[256,512]{1,0:T(8,128)S(1)} collective-permute-done((f32[256,512]{1,0:T(8,128)S(1)}, f32[256,512]{1,0:T(8,128)S(1)}, u32[]{:S(2)}, u32[]{:S(2)}) %collective-permute-start.10) | collective-permute-done | bytes 524320 | tf_op jit(solution)/shard_map/ppermute | solution.py:15
  214.2 2.0 gather_fusion.3
  216.2 2.0 gather_fusion.2
  218.2 4.0 %fusion.10 = f32[4,256,512]{2,1,0:T(8,128)S(1)} fusion(f32[4,256,256]{2,1,0:T(8,128)S(1)} %copy-done.1, f32[4,256,512]{2,1,0:T(8,128)} %gather_fusion.3, pred[4]{0:T(512)(128)(4,1)S(1)} %compare_and_fusion), kind=kOutput, calls=%fused_computation.22 | convolution fusion | flops 1611137024 | bytes 5242884 | tf_op jit(solution)/shard_map/pab,pac->pbc/dot_general | solution.py:90
  222.2 3.3 %fusion.4 = f32[4,256,512]{2,0,1:T(4,128)S(1)} fusion(f32[4,256,512]{2,1,0:T(8,128)S(1)} %fusion.10, f32[4]{0:T(128)S(1)} %get-tuple-element.39, s32[4]{0:T(128)S(1)} %bitcast.114), kind=kOutput, calls=%fused_computation.14 | convolution fusion | flops 25690128 | bytes 4194336 | tf_op jit(solution)/shard_map/pl,pac->lac/dot_general | solution.py:105
  225.6 2.1 fusion.12
  227.7 3.2 %fusion.5 = f32[4,256,512]{2,0,1:T(4,128)S(1)} fusion(f32[4,256,512]{2,1,0:T(8,128)S(1)} %fusion.12, s32[4]{0:T(128)S(1)} %bitcast.112), kind=kOutput, calls=%fused_computation.15 | convolution fusion | flops 25165840 | bytes 4194320 | tf_op jit(solution)/shard_map/pl,pac->lac/dot_general | solution.py:98
  232.3 1.6 collective-permute-start.12
  233.9 7.3 %collective-permute-start.14 = (f32[256,512]{1,0:T(8,128)S(1)}, f32[256,512]{1,0:T(8,128)S(1)}, u32[]{:S(2)}, u32[]{:S(2)}) collective-permute-start(f32[256,512]{1,0:T(8,128)S(1)} %get-tuple-element.44), channel_id=1, source_target_pairs={{0,6},{2,8},{4,10},{6,12},{8,14},{10,16},{12,18},{14,20},{16,22},{... | collective-permute-start | bytes 1572872 | tf_op jit(solution)/shard_map/ppermute | solution.py:15
  241.2 4.8 %collective-permute-start.13 = (f32[256,512]{1,0:T(8,128)S(1)}, f32[256,512]{1,0:T(8,128)S(1)}, u32[]{:S(2)}, u32[]{:S(2)}) collective-permute-start(f32[256,512]{1,0:T(8,128)S(1)} %get-tuple-element.45), channel_id=1, source_target_pairs={{0,4},{2,6},{4,8},{6,10},{8,12},{10,14},{12,16},{14,18},{16,20},{1... | collective-permute-start | bytes 1572872 | tf_op jit(solution)/shard_map/ppermute | solution.py:15
  246.0 8.8 %collective-permute-done.12 = f32[256,512]{1,0:T(8,128)S(1)} collective-permute-done((f32[256,512]{1,0:T(8,128)S(1)}, f32[256,512]{1,0:T(8,128)S(1)}, u32[]{:S(2)}, u32[]{:S(2)}) %collective-permute-start.12) | collective-permute-done | bytes 524320 | tf_op jit(solution)/shard_map/ppermute | solution.py:15
  254.8 6.1 %collective-permute-done.14 = f32[256,512]{1,0:T(8,128)S(1)} collective-permute-done((f32[256,512]{1,0:T(8,128)S(1)}, f32[256,512]{1,0:T(8,128)S(1)}, u32[]{:S(2)}, u32[]{:S(2)}) %collective-permute-start.14) | collective-permute-done | bytes 524320 | tf_op jit(solution)/shard_map/ppermute | solution.py:15
  260.9 19.1 %collective-permute-done.13 = f32[256,512]{1,0:T(8,128)S(1)} collective-permute-done((f32[256,512]{1,0:T(8,128)S(1)}, f32[256,512]{1,0:T(8,128)S(1)}, u32[]{:S(2)}, u32[]{:S(2)}) %collective-permute-start.13) | collective-permute-done | bytes 524320 | tf_op jit(solution)/shard_map/ppermute | solution.py:15
  (59 shorter events, 7.4 us)
Async XLA Ops:
  6.5 49.8 %copy-start = (f32[8]{0:T(128)S(1)}, f32[8]{0:T(128)}, u32[]{:S(2)}) copy-start(f32[8]{0:T(128)} %param.14) | copy-start | bytes 100
  6.5 9.3 %copy-start.8 = (f32[256,512]{1,0:T(8,128)S(1)}, f32[256,512]{1,0:T(8,128)}, u32[]{:S(2)}) copy-start(f32[256,512]{1,0:T(8,128)} %param.17) | copy-start | bytes 1572868
  6.5 15.4 %copy-start.9 = (s32[4,3]{1,0:T(4,128)S(1)}, s32[4,3]{1,0:T(4,128)}, u32[]{:S(2)}) copy-start(s32[4,3]{1,0:T(4,128)} %param.12) | copy-start | bytes 148
  8.5 21.4 %all-to-all-start = ((f32[32,16,256]{2,0,1:T(8,128)}), f32[32,16,256]{2,0,1:T(8,128)S(1)}, u32[]{:S(2)}, u32[]{:S(2)}) async-start(f32[32,16,256]{2,0,1:T(8,128)} %bitcast.87), calls=%async_computation | async-start | bytes 1048576 | tf_op jit(solution)/shard_map/all_to_all | solution.py:40
  15.8 117.9 %all-reduce.2.cloned.1.call-start = ((), (), s32[]{:S(2)}) async-start(), calls=%async_computation.1 | async-start | bytes 2097152 | tf_op jit(solution)/shard_map/psum | solution.py:72
  15.9 81.9 %collective-permute-start.4 = (f32[256,512]{1,0:T(8,128)S(1)}, f32[256,512]{1,0:T(8,128)}, u32[]{:S(2)}, u32[]{:S(2)}) collective-permute-start(f32[256,512]{1,0:T(8,128)S(1)} %copy-done.8), channel_id=1, source_target_pairs={{0,28},{2,30},{4,0},{6,2},{8,4},{10,6},{12,8},{14,10},{16,12},{18,... | collective-permute-start | bytes 1572872 | tf_op jit(solution)/shard_map/ppermute | solution.py:15
  20.1 77.6 %collective-permute-start.3 = (f32[256,512]{1,0:T(8,128)S(1)}, f32[256,512]{1,0:T(8,128)}, u32[]{:S(2)}, u32[]{:S(2)}) collective-permute-start(f32[256,512]{1,0:T(8,128)S(1)} %copy-done.8), channel_id=1, source_target_pairs={{0,30},{2,0},{4,2},{6,4},{8,6},{10,8},{12,10},{14,12},{16,14},{18,... | collective-permute-start | bytes 1572872 | tf_op jit(solution)/shard_map/ppermute | solution.py:15
  29.9 35.7 %collective-permute-start.2 = (f32[512,256]{1,0:T(8,128)S(1)}, f32[512,256]{1,0:T(8,128)S(1)}, u32[]{:S(2)}, u32[]{:S(2)}) collective-permute-start(f32[512,256]{1,0:T(8,128)S(1)} %bitcast.103), channel_id=1, source_target_pairs={{0,26},{2,28},{4,30},{6,0},{8,2},{10,4},{12,6},{14,8},{16,10},{18,... | collective-permute-start | bytes 1572872 | tf_op jit(solution)/shard_map/ppermute | solution.py:15
  53.3 23.5 %collective-permute-start.1 = (f32[512,256]{1,0:T(8,128)S(1)}, f32[512,256]{1,0:T(8,128)S(1)}, u32[]{:S(2)}, u32[]{:S(2)}) collective-permute-start(f32[512,256]{1,0:T(8,128)S(1)} %bitcast.104), channel_id=1, source_target_pairs={{0,28},{2,30},{4,0},{6,2},{8,4},{10,6},{12,8},{14,10},{16,12},{18,... | collective-permute-start | bytes 1572872 | tf_op jit(solution)/shard_map/ppermute | solution.py:15
  55.0 24.8 %collective-permute-start = (f32[512,256]{1,0:T(8,128)S(1)}, f32[512,256]{1,0:T(8,128)S(1)}, u32[]{:S(2)}, u32[]{:S(2)}) collective-permute-start(f32[512,256]{1,0:T(8,128)S(1)} %bitcast.105), channel_id=1, source_target_pairs={{0,30},{2,0},{4,2},{6,4},{8,6},{10,8},{12,10},{14,12},{16,14},{18,... | collective-permute-start | bytes 1572872 | tf_op jit(solution)/shard_map/ppermute | solution.py:15
  65.6 35.9 %collective-permute-start.5 = (f32[256,512]{1,0:T(8,128)S(1)}, f32[256,512]{1,0:T(8,128)}, u32[]{:S(2)}, u32[]{:S(2)}) collective-permute-start(f32[256,512]{1,0:T(8,128)S(1)} %copy-done.8), channel_id=1, source_target_pairs={{0,26},{2,28},{4,30},{6,0},{8,2},{10,4},{12,6},{14,8},{16,10},{18,... | collective-permute-start | bytes 1572872 | tf_op jit(solution)/shard_map/ppermute | solution.py:15
  137.9 3.4 %copy-start.1 = (f32[4,256,256]{2,1,0:T(8,128)S(1)}, f32[4,256,256]{2,1,0:T(8,128)}, u32[]{:S(2)}) copy-start(f32[4,256,256]{2,1,0:T(8,128)} %all-reduce.2.cloned.1.call-done) | copy-start | bytes 3145732
  137.9 3.4 %copy-start.2 = (f32[4,256,512]{2,1,0:T(8,128)S(1)}, f32[4,256,512]{2,1,0:T(8,128)}, u32[]{:S(2)}) copy-start(f32[4,256,512]{2,1,0:T(8,128)} %gather_fusion) | copy-start | bytes 6291460
  148.7 28.2 %copy-start.6 = (f32[256,512]{1,0:T(8,128)S(1)}, f32[256,512]{1,0:T(8,128)}, u32[]{:S(2)}) copy-start(f32[256,512]{1,0:T(8,128)} %param.16) | copy-start | bytes 1572868
  148.9 24.4 %collective-permute-start.7 = (f32[256,512]{1,0:T(8,128)S(1)}, f32[256,512]{1,0:T(8,128)S(1)}, u32[]{:S(2)}, u32[]{:S(2)}) collective-permute-start(f32[256,512]{1,0:T(8,128)S(1)} %bitcast.110), channel_id=1, source_target_pairs={{0,4},{2,6},{4,8},{6,10},{8,12},{10,14},{12,16},{14,18},{16,20},{1... | collective-permute-start | bytes 1572872 | tf_op jit(solution)/shard_map/ppermute | solution.py:15
  150.4 26.6 %collective-permute-start.8 = (f32[256,512]{1,0:T(8,128)S(1)}, f32[256,512]{1,0:T(8,128)S(1)}, u32[]{:S(2)}, u32[]{:S(2)}) collective-permute-start(f32[256,512]{1,0:T(8,128)S(1)} %bitcast.109), channel_id=1, source_target_pairs={{0,6},{2,8},{4,10},{6,12},{8,14},{10,16},{12,18},{14,20},{16,22},{... | collective-permute-start | bytes 1572872 | tf_op jit(solution)/shard_map/ppermute | solution.py:15
  151.9 25.1 %collective-permute-start.6 = (f32[256,512]{1,0:T(8,128)S(1)}, f32[256,512]{1,0:T(8,128)S(1)}, u32[]{:S(2)}, u32[]{:S(2)}) collective-permute-start(f32[256,512]{1,0:T(8,128)S(1)} %bitcast.108), channel_id=1, source_target_pairs={{0,2},{2,4},{4,6},{6,8},{8,10},{10,12},{12,14},{14,16},{16,18},{18... | collective-permute-start | bytes 1572872 | tf_op jit(solution)/shard_map/ppermute | solution.py:15
  177.3 36.9 %copy-start.4 = (f32[256,512]{1,0:T(8,128)}, f32[256,512]{1,0:T(8,128)S(1)}, u32[]{:S(2)}) copy-start(f32[256,512]{1,0:T(8,128)S(1)} %fusion.45) | copy-start | bytes 1572868
  177.3 24.7 %collective-permute-start.11 = (f32[256,512]{1,0:T(8,128)S(1)}, f32[256,512]{1,0:T(8,128)S(1)}, u32[]{:S(2)}, u32[]{:S(2)}) collective-permute-start(f32[256,512]{1,0:T(8,128)S(1)} %fusion.45), channel_id=1, source_target_pairs={{0,26},{2,28},{4,30},{6,0},{8,2},{10,4},{12,6},{14,8},{16,10},{18,... | collective-permute-start | bytes 1572872 | tf_op jit(solution)/shard_map/ppermute | solution.py:15
  181.0 33.0 %collective-permute-start.10 = (f32[256,512]{1,0:T(8,128)S(1)}, f32[256,512]{1,0:T(8,128)S(1)}, u32[]{:S(2)}, u32[]{:S(2)}) collective-permute-start(f32[256,512]{1,0:T(8,128)S(1)} %fusion.45), channel_id=1, source_target_pairs={{0,28},{2,30},{4,0},{6,2},{8,4},{10,6},{12,8},{14,10},{16,12},{18,... | collective-permute-start | bytes 1572872 | tf_op jit(solution)/shard_map/ppermute | solution.py:15
  192.5 21.5 %collective-permute-start.9 = (f32[256,512]{1,0:T(8,128)S(1)}, f32[256,512]{1,0:T(8,128)S(1)}, u32[]{:S(2)}, u32[]{:S(2)}) collective-permute-start(f32[256,512]{1,0:T(8,128)S(1)} %fusion.45), channel_id=1, source_target_pairs={{0,30},{2,0},{4,2},{6,4},{8,6},{10,8},{12,10},{14,12},{16,14},{18,... | collective-permute-start | bytes 1572872 | tf_op jit(solution)/shard_map/ppermute | solution.py:15
  222.2 3.4 %copy-start.3 = (f32[4,256,512]{2,1,0:T(8,128)S(1)}, f32[4,256,512]{2,1,0:T(8,128)}, u32[]{:S(2)}) copy-start(f32[4,256,512]{2,1,0:T(8,128)} %gather_fusion.2) | copy-start | bytes 6291460
  232.2 47.8 %copy-start.5 = (f32[256,512]{1,0:T(8,128)S(1)}, f32[256,512]{1,0:T(8,128)}, u32[]{:S(2)}) copy-start(f32[256,512]{1,0:T(8,128)} %copy-done.4) | copy-start | bytes 1572868
  232.2 47.8 %copy-start.7 = (f32[256,512]{1,0:T(8,128)S(1)}, f32[256,512]{1,0:T(8,128)}, u32[]{:S(2)}) copy-start(f32[256,512]{1,0:T(8,128)} %param.16) | copy-start | bytes 1572868
  232.3 22.4 %collective-permute-start.12 = (f32[256,512]{1,0:T(8,128)S(1)}, f32[256,512]{1,0:T(8,128)S(1)}, u32[]{:S(2)}, u32[]{:S(2)}) collective-permute-start(f32[256,512]{1,0:T(8,128)S(1)} %get-tuple-element.43), channel_id=1, source_target_pairs={{0,2},{2,4},{4,6},{6,8},{8,10},{10,12},{12,14},{14,16},{16,18},{18... | collective-permute-start | bytes 1572872 | tf_op jit(solution)/shard_map/ppermute | solution.py:15
  233.9 27.0 %collective-permute-start.14 = (f32[256,512]{1,0:T(8,128)S(1)}, f32[256,512]{1,0:T(8,128)S(1)}, u32[]{:S(2)}, u32[]{:S(2)}) collective-permute-start(f32[256,512]{1,0:T(8,128)S(1)} %get-tuple-element.44), channel_id=1, source_target_pairs={{0,6},{2,8},{4,10},{6,12},{8,14},{10,16},{12,18},{14,20},{16,22},{... | collective-permute-start | bytes 1572872 | tf_op jit(solution)/shard_map/ppermute | solution.py:15
  241.2 38.8 %collective-permute-start.13 = (f32[256,512]{1,0:T(8,128)S(1)}, f32[256,512]{1,0:T(8,128)S(1)}, u32[]{:S(2)}, u32[]{:S(2)}) collective-permute-start(f32[256,512]{1,0:T(8,128)S(1)} %get-tuple-element.45), channel_id=1, source_target_pairs={{0,4},{2,6},{4,8},{6,10},{8,12},{10,14},{12,16},{14,18},{16,20},{1... | collective-permute-start | bytes 1572872 | tf_op jit(solution)/shard_map/ppermute | solution.py:15
Sparse Core Ops, SparseCore 0:
  97.8 35.9 all-reduce.1
where the time goes:
time: 288 us
  waiting for transfers between devices  133 us (46%)
  starting transfers between devices  79 us (27%)
  matrix products  33.3 us (12%)
  between operations  15 us (5%)
  local copies, waits for them, and re-layouts  14.9 us (5%)
  other arithmetic  7.2 us (2%)
  loops' own time  5.42 us (2%)
    ppermute x15, waiting for transfers between devices, shifted(): lax.ppermute(array, axis, [(i, (i + by) % count) for i in range(count)])  99 us
    ppermute x15, starting transfers between devices, shifted(): lax.ppermute(array, axis, [(i, (i + by) % count) for i in range(count)])  71.7 us
    psum x1, waiting for transfers between devices, per_device(): tiles = lax.psum(partial_value, 'mem')  26.6 us
    dot_general x2, matrix products, per_device(): jnp.einsum('pab,pac->pbc', tiles, own_blocks, precision=lax.Precision.HIG...  8.13 us
    all_to_all x1, waiting for transfers between devices, per_device(): lax.all_to_all(perturb, 'space', split_axis=1, concat_axis=0, tiled=True)  7.55 us
    all_to_all x1, starting transfers between devices, per_device(): lax.all_to_all(perturb, 'space', split_axis=1, concat_axis=0, tiled=True)  7.31 us
    dot_general x2, matrix products, per_device(): jnp.einsum('pl,pac->lac', first_select, forward, precision=lax.Precision....  7.02 us
    dot_general x4, matrix products, build_tile(): jnp.einsum('ma,mb->ab', first_cols, second_cols, precision=lax.Precision....  7.01 us
  transfers between devices with their start and end apart: 17, of which 13 were waited for; matrix products, arithmetic and copies ran while one was open for 6% of the time, Pallas kernels for 0%

commit v1 on v0

--- a/solution.py
+++ b/solution.py
@@ -8,6 +8,12 @@
 REACH_DEV = 3
 NBANDS = 8
 ITERS = 2
+_bind_bands = lambda slab_in, ndim_at, dimension_no: jnp.concatenate(
+    lax.all_to_all(
+        jnp.stack(jnp.split(slab_in, lax.axis_size("space"), ndim_at), axis=0), "space", 0, 0
+    ),
+    axis=dimension_no,
+)
 
 
 def shifted(array, axis, by):
@@ -37,7 +43,7 @@
 
 
 def per_device(perturb, pair_list, pair_count, band_weight, cov_scale, target, first_guess):
-    own_members = lax.all_to_all(perturb, "space", split_axis=1, concat_axis=0, tiled=True)
+    own_members = _bind_bands(perturb, 1, 0)
     rows_dev = own_members.shape[1]
     blocks_dev = rows_dev // BLOCK
     blocks_near = (REACH_DEV + 1) * blocks_dev

time: 288 us -> 309 us (1.073)
  local copies, waits for them, and re-layouts: 14.9 us -> 34.7 us
    unnamed x25 -> x40, local copies, waits for them, and re-layouts: 0.34 us -> 21 us
where the time goes in v1:
time: 309 us; the launch traced here: 307 us
  waiting for transfers between devices  133 us (43%)
  starting transfers between devices  79 us (26%)
  local copies, waits for them, and re-layouts  34.7 us (11%)
  matrix products  33.2 us (11%)
  between operations  15 us (5%)
  other arithmetic  7.21 us (2%)
  loops' own time  4.95 us (2%)
    ppermute x15, waiting for transfers between devices, shifted(): lax.ppermute(array, axis, [(i, (i + by) % count) for i in range(count)])  99.7 us
    ppermute x15, starting transfers between devices, shifted(): lax.ppermute(array, axis, [(i, (i + by) % count) for i in range(count)])  71.7 us
    psum x1, waiting for transfers between devices, per_device(): tiles = lax.psum(partial_value, 'mem')  25.9 us
    unnamed x40, local copies, waits for them, and re-layouts  21 us
    dot_general x2, matrix products, per_device(): jnp.einsum('pab,pac->pbc', tiles, own_blocks, precision=lax.Precision.HIG...  8.13 us
    all_to_all x1, waiting for transfers between devices, lax.all_to_all(jnp.stack(jnp.split(slab_in, lax.axis_size('space'), ndim_...  7.58 us
    all_to_all x1, starting transfers between devices, lax.all_to_all(jnp.stack(jnp.split(slab_in, lax.axis_size('space'), ndim_...  7.31 us
    dot_general x2, matrix products, per_device(): jnp.einsum('pl,pac->lac', first_select, forward, precision=lax.Precision....  7.02 us
  transfers between devices with their start and end apart: 17, of which 13 were waited for; matrix products, arithmetic and copies ran while one was open for 6% of the time, Pallas kernels for 0%

profile of v1, /device:TPU:2, one launch (start us, length us, event | category | flops | bytes accessed | tf_op | source)
XLA Modules:
  0.0 307.3 jit_solution(348701280800497161)
XLA Ops:
  6.5 1.4 constant_dynamic-update-slice_fusion.15
  19.0 1.4 constant_dynamic-update-slice_fusion.6
  28.6 7.3 %all-to-all-start = ((f32[16,32,256]{2,1,0:T(8,128)}), f32[16,32,256]{2,1,0:T(8,128)S(1)}, u32[]{:S(2)}, u32[]{:S(2)}) async-start(f32[16,32,256]{2,1,0:T(8,128)} %constant_dynamic-update-slice_fusion), calls=%async_computation | async-start | bytes 1048576 | tf_op jit(solution)/shard_map/all_to_all | solution.py:12
  35.9 4.2 %collective-permute-start.4 = (f32[256,512]{1,0:T(8,128)S(1)}, f32[256,512]{1,0:T(8,128)}, u32[]{:S(2)}, u32[]{:S(2)}) collective-permute-start(f32[256,512]{1,0:T(8,128)S(1)} %copy-done.8), channel_id=1, source_target_pairs={{0,28},{2,30},{4,0},{6,2},{8,4},{10,6},{12,8},{14,10},{16,12},{18,... | collective-permute-start | bytes 1572872 | tf_op jit(solution)/shard_map/ppermute | solution.py:21
  42.4 7.6 %all-to-all-done = f32[16,32,256]{2,1,0:T(8,128)S(1)} async-done(((f32[16,32,256]{2,1,0:T(8,128)}), f32[16,32,256]{2,1,0:T(8,128)S(1)}, u32[]{:S(2)}, u32[]{:S(2)}) %all-to-all-start) | async-done | bytes 524320 | tf_op jit(solution)/shard_map/all_to_all | solution.py:12
  50.0 23.3 %collective-permute-start.2 = (f32[512,256]{1,0:T(8,128)S(1)}, f32[512,256]{1,0:T(8,128)S(1)}, u32[]{:S(2)}, u32[]{:S(2)}) collective-permute-start(f32[512,256]{1,0:T(8,128)S(1)} %bitcast.129), channel_id=1, source_target_pairs={{0,26},{2,28},{4,30},{6,0},{8,2},{10,4},{12,6},{14,8},{16,10},{18,... | collective-permute-start | bytes 1572872 | tf_op jit(solution)/shard_map/ppermute | solution.py:21
  73.3 1.8 collective-permute-start.1
  76.7 9.0 %collective-permute-done.2 = f32[512,256]{1,0:T(8,128)S(1)} collective-permute-done((f32[512,256]{1,0:T(8,128)S(1)}, f32[512,256]{1,0:T(8,128)S(1)}, u32[]{:S(2)}, u32[]{:S(2)}) %collective-permute-start.2) | collective-permute-done | bytes 524320 | tf_op jit(solution)/shard_map/ppermute | solution.py:21
  85.7 6.2 %collective-permute-start.5 = (f32[256,512]{1,0:T(8,128)S(1)}, f32[256,512]{1,0:T(8,128)}, u32[]{:S(2)}, u32[]{:S(2)}) collective-permute-start(f32[256,512]{1,0:T(8,128)S(1)} %copy-done.8), channel_id=1, source_target_pairs={{0,26},{2,28},{4,30},{6,0},{8,2},{10,4},{12,6},{14,8},{16,10},{18,... | collective-permute-start | bytes 1572872 | tf_op jit(solution)/shard_map/ppermute | solution.py:21
  91.9 4.9 %collective-permute-done.1 = f32[512,256]{1,0:T(8,128)S(1)} collective-permute-done((f32[512,256]{1,0:T(8,128)S(1)}, f32[512,256]{1,0:T(8,128)S(1)}, u32[]{:S(2)}, u32[]{:S(2)}) %collective-permute-start.1) | collective-permute-done | bytes 524320 | tf_op jit(solution)/shard_map/ppermute | solution.py:21
  96.8 3.1 %collective-permute-done = f32[512,256]{1,0:T(8,128)S(1)} collective-permute-done((f32[512,256]{1,0:T(8,128)S(1)}, f32[512,256]{1,0:T(8,128)S(1)}, u32[]{:S(2)}, u32[]{:S(2)}) %collective-permute-start) | collective-permute-done | bytes 524320 | tf_op jit(solution)/shard_map/ppermute | solution.py:21
  100.2 14.3 %while.10 = (s32[]{:T(128)}, f32[4,256,256]{2,1,0:T(8,128)}, s32[4,2]{0,1:T(2,128)S(1)}, f32[512,1024]{1,0:T(8,128)S(1)}, s32[]{:T(128)}, /*index=5*/s32[1,1]{0,1:T(1,128)}, s32[]{:T(128)}, s32[]{:T(128)}) while((s32[]{:T(128)}, f32[4,256,256]{2,1,0:T(8,128)}, s32[4,2]{0,1:T(2,128)S(1)}, f32[512,1024]{1,0:T(8,128)S(1)}, s32[]{:T(128)}, ...), condition=%wide.region_1.2_spmd, body=%wide.region_0.1_spmd.sunk | while | flops 402653184 | bytes 1310953 | solution.py:76
  102.1 1.7 fusion.79
  105.6 1.7 fusion.79
  109.2 1.8 fusion.79
  112.8 1.8 fusion.79
  114.6 2.4 broadcast_multiply_fusion
  117.1 4.5 %collective-permute-done.5 = f32[256,512]{1,0:T(8,128)} collective-permute-done((f32[256,512]{1,0:T(8,128)S(1)}, f32[256,512]{1,0:T(8,128)}, u32[]{:S(2)}, u32[]{:S(2)}) %collective-permute-start.5) | collective-permute-done | bytes 524320 | tf_op jit(solution)/shard_map/ppermute | solution.py:21
  121.5 1.6 pad_maximum_fusion.1
  123.1 2.0 gather_fusion.1
  125.1 2.0 gather_fusion
  127.2 25.9 %all-reduce.2.cloned.1.call-done = f32[4,256,256]{2,1,0:T(8,128)} async-done(((f32[4,256,256]{2,1,0:T(8,128)}), f32[4,256,256]{2,1,0:T(8,128)}) %all-reduce.2.cloned.1.call-update) | async-done | bytes 1048592 | tf_op jit(solution)/shard_map/psum | solution.py:78
  153.0 4.2 %fusion.14 = f32[4,256,512]{2,1,0:T(8,128)S(1)} fusion(f32[4,256,256]{2,1,0:T(8,128)} %all-reduce.2.cloned.1.call-done, f32[4,256,512]{2,1,0:T(8,128)} %gather_fusion.1, pred[4]{0:T(512)(128)(4,1)S(1)} %compare_and_fusion), kind=kOutput, calls=%fused_computation.26 | convolution fusion | flops 1611137024 | bytes 5242884 | tf_op jit(solution)/shard_map/pab,pac->pbc/dot_general | solution.py:96
  157.3 3.3 %fusion.7 = f32[4,256,512]{2,0,1:T(4,128)S(1)} fusion(f32[4,256,512]{2,1,0:T(8,128)S(1)} %fusion.14, f32[4]{0:T(128)S(1)} %get-tuple-element.39, s32[4]{0:T(128)S(1)} %bitcast.138), kind=kOutput, calls=%fused_computation.18 | convolution fusion | flops 25690128 | bytes 4194336 | tf_op jit(solution)/shard_map/pl,pac->lac/dot_general | solution.py:111
  160.6 2.1 fusion.16
  162.7 3.8 %fusion.18 = f32[4,256,512]{2,0,1:T(4,128)S(1)} fusion(f32[4,256,512]{2,0,1:T(4,128)S(1)} %fusion.7, f32[4,256,512]{2,1,0:T(8,128)S(1)} %fusion.16, s32[4]{0:T(128)S(1)} %bitcast.136), kind=kOutput, calls=%fused_computation.30 | convolution fusion | flops 25690128 | bytes 6291472 | tf_op jit(solution)/shard_map/pl,pac->lac/dot_general | solution.py:104
  166.5 1.5 fusion.67
  168.2 1.5 collective-permute-start.7
  169.7 1.5 collective-permute-start.8
  171.2 2.4 collective-permute-start.6
  173.6 19.0 %collective-permute-done.7 = f32[256,512]{1,0:T(8,128)S(1)} collective-permute-done((f32[256,512]{1,0:T(8,128)S(1)}, f32[256,512]{1,0:T(8,128)S(1)}, u32[]{:S(2)}, u32[]{:S(2)}) %collective-permute-start.7) | collective-permute-done | bytes 524320 | tf_op jit(solution)/shard_map/ppermute | solution.py:21
  192.6 3.7 %collective-permute-done.8 = f32[256,512]{1,0:T(8,128)S(1)} collective-permute-done((f32[256,512]{1,0:T(8,128)S(1)}, f32[256,512]{1,0:T(8,128)S(1)}, u32[]{:S(2)}, u32[]{:S(2)}) %collective-permute-start.8) | collective-permute-done | bytes 524320 | tf_op jit(solution)/shard_map/ppermute | solution.py:21
  196.7 3.7 %collective-permute-start.11 = (f32[256,512]{1,0:T(8,128)S(1)}, f32[256,512]{1,0:T(8,128)S(1)}, u32[]{:S(2)}, u32[]{:S(2)}) collective-permute-start(f32[256,512]{1,0:T(8,128)S(1)} %fusion.45), channel_id=1, source_target_pairs={{0,26},{2,28},{4,30},{6,0},{8,2},{10,4},{12,6},{14,8},{16,10},{18,... | collective-permute-start | bytes 1572872 | tf_op jit(solution)/shard_map/ppermute | solution.py:21
  200.3 11.5 %collective-permute-start.10 = (f32[256,512]{1,0:T(8,128)S(1)}, f32[256,512]{1,0:T(8,128)S(1)}, u32[]{:S(2)}, u32[]{:S(2)}) collective-permute-start(f32[256,512]{1,0:T(8,128)S(1)} %fusion.45), channel_id=1, source_target_pairs={{0,28},{2,30},{4,0},{6,2},{8,4},{10,6},{12,8},{14,10},{16,12},{18,... | collective-permute-start | bytes 1572872 | tf_op jit(solution)/shard_map/ppermute | solution.py:21
  211.9 9.5 %collective-permute-done.11 = f32[256,512]{1,0:T(8,128)S(1)} collective-permute-done((f32[256,512]{1,0:T(8,128)S(1)}, f32[256,512]{1,0:T(8,128)S(1)}, u32[]{:S(2)}, u32[]{:S(2)}) %collective-permute-start.11) | collective-permute-done | bytes 524320 | tf_op jit(solution)/shard_map/ppermute | solution.py:21
  221.3 12.0 %collective-permute-done.10 = f32[256,512]{1,0:T(8,128)S(1)} collective-permute-done((f32[256,512]{1,0:T(8,128)S(1)}, f32[256,512]{1,0:T(8,128)S(1)}, u32[]{:S(2)}, u32[]{:S(2)}) %collective-permute-start.10) | collective-permute-done | bytes 524320 | tf_op jit(solution)/shard_map/ppermute | solution.py:21
  233.5 2.0 gather_fusion.3
  235.6 2.0 gather_fusion.2
  237.6 4.0 %fusion.10 = f32[4,256,512]{2,1,0:T(8,128)S(1)} fusion(f32[4,256,256]{2,1,0:T(8,128)S(1)} %copy-done.1, f32[4,256,512]{2,1,0:T(8,128)} %gather_fusion.3, pred[4]{0:T(512)(128)(4,1)S(1)} %compare_and_fusion), kind=kOutput, calls=%fused_computation.22 | convolution fusion | flops 1611137024 | bytes 5242884 | tf_op jit(solution)/shard_map/pab,pac->pbc/dot_general | solution.py:96
  241.5 3.3 %fusion.4 = f32[4,256,512]{2,0,1:T(4,128)S(1)} fusion(f32[4,256,512]{2,1,0:T(8,128)S(1)} %fusion.10, f32[4]{0:T(128)S(1)} %get-tuple-element.39, s32[4]{0:T(128)S(1)} %bitcast.139), kind=kOutput, calls=%fused_computation.14 | convolution fusion | flops 25690128 | bytes 4194336 | tf_op jit(solution)/shard_map/pl,pac->lac/dot_general | solution.py:111
  244.9 2.1 fusion.12
  247.0 3.2 %fusion.5 = f32[4,256,512]{2,0,1:T(4,128)S(1)} fusion(f32[4,256,512]{2,1,0:T(8,128)S(1)} %fusion.12, s32[4]{0:T(128)S(1)} %bitcast.137), kind=kOutput, calls=%fused_computation.15 | convolution fusion | flops 25165840 | bytes 4194320 | tf_op jit(solution)/shard_map/pl,pac->lac/dot_general | solution.py:104
  251.6 1.6 collective-permute-start.12
  253.2 7.3 %collective-permute-start.14 = (f32[256,512]{1,0:T(8,128)S(1)}, f32[256,512]{1,0:T(8,128)S(1)}, u32[]{:S(2)}, u32[]{:S(2)}) collective-permute-start(f32[256,512]{1,0:T(8,128)S(1)} %get-tuple-element.44), channel_id=1, source_target_pairs={{0,6},{2,8},{4,10},{6,12},{8,14},{10,16},{12,18},{14,20},{16,22},{... | collective-permute-start | bytes 1572872 | tf_op jit(solution)/shard_map/ppermute | solution.py:21
  260.5 4.8 %collective-permute-start.13 = (f32[256,512]{1,0:T(8,128)S(1)}, f32[256,512]{1,0:T(8,128)S(1)}, u32[]{:S(2)}, u32[]{:S(2)}) collective-permute-start(f32[256,512]{1,0:T(8,128)S(1)} %get-tuple-element.45), channel_id=1, source_target_pairs={{0,4},{2,6},{4,8},{6,10},{8,12},{10,14},{12,16},{14,18},{16,20},{1... | collective-permute-start | bytes 1572872 | tf_op jit(solution)/shard_map/ppermute | solution.py:21
  265.3 8.8 %collective-permute-done.12 = f32[256,512]{1,0:T(8,128)S(1)} collective-permute-done((f32[256,512]{1,0:T(8,128)S(1)}, f32[256,512]{1,0:T(8,128)S(1)}, u32[]{:S(2)}, u32[]{:S(2)}) %collective-permute-start.12) | collective-permute-done | bytes 524320 | tf_op jit(solution)/shard_map/ppermute | solution.py:21
  274.1 6.1 %collective-permute-done.14 = f32[256,512]{1,0:T(8,128)S(1)} collective-permute-done((f32[256,512]{1,0:T(8,128)S(1)}, f32[256,512]{1,0:T(8,128)S(1)}, u32[]{:S(2)}, u32[]{:S(2)}) %collective-permute-start.14) | collective-permute-done | bytes 524320 | tf_op jit(solution)/shard_map/ppermute | solution.py:21
  280.2 19.1 %collective-permute-done.13 = f32[256,512]{1,0:T(8,128)S(1)} collective-permute-done((f32[256,512]{1,0:T(8,128)S(1)}, f32[256,512]{1,0:T(8,128)S(1)}, u32[]{:S(2)}, u32[]{:S(2)}) %collective-permute-start.13) | collective-permute-done | bytes 524320 | tf_op jit(solution)/shard_map/ppermute | solution.py:21
  (73 shorter events, 27.6 us)
Async XLA Ops:
  6.5 69.9 %copy-start = (f32[8]{0:T(128)S(1)}, f32[8]{0:T(128)}, u32[]{:S(2)}) copy-start(f32[8]{0:T(128)} %param.14) | copy-start | bytes 100
  6.5 29.4 %copy-start.8 = (f32[256,512]{1,0:T(8,128)S(1)}, f32[256,512]{1,0:T(8,128)}, u32[]{:S(2)}) copy-start(f32[256,512]{1,0:T(8,128)} %param.17) | copy-start | bytes 1572868
  6.5 35.5 %copy-start.9 = (s32[4,3]{1,0:T(4,128)S(1)}, s32[4,3]{1,0:T(4,128)}, u32[]{:S(2)}) copy-start(s32[4,3]{1,0:T(4,128)} %param.12) | copy-start | bytes 148
  28.6 21.4 %all-to-all-start = ((f32[16,32,256]{2,1,0:T(8,128)}), f32[16,32,256]{2,1,0:T(8,128)S(1)}, u32[]{:S(2)}, u32[]{:S(2)}) async-start(f32[16,32,256]{2,1,0:T(8,128)} %constant_dynamic-update-slice_fusion), calls=%async_computation | async-start | bytes 1048576 | tf_op jit(solution)/shard_map/all_to_all | solution.py:12
  35.9 117.2 %all-reduce.2.cloned.1.call-start = ((), (), s32[]{:S(2)}) async-start(), calls=%async_computation.1 | async-start | bytes 2097152 | tf_op jit(solution)/shard_map/psum | solution.py:78
  35.9 81.1 %collective-permute-start.4 = (f32[256,512]{1,0:T(8,128)S(1)}, f32[256,512]{1,0:T(8,128)}, u32[]{:S(2)}, u32[]{:S(2)}) collective-permute-start(f32[256,512]{1,0:T(8,128)S(1)} %copy-done.8), channel_id=1, source_target_pairs={{0,28},{2,30},{4,0},{6,2},{8,4},{10,6},{12,8},{14,10},{16,12},{18,... | collective-permute-start | bytes 1572872 | tf_op jit(solution)/shard_map/ppermute | solution.py:21
  40.2 76.9 %collective-permute-start.3 = (f32[256,512]{1,0:T(8,128)S(1)}, f32[256,512]{1,0:T(8,128)}, u32[]{:S(2)}, u32[]{:S(2)}) collective-permute-start(f32[256,512]{1,0:T(8,128)S(1)} %copy-done.8), channel_id=1, source_target_pairs={{0,30},{2,0},{4,2},{6,4},{8,6},{10,8},{12,10},{14,12},{16,14},{18,... | collective-permute-start | bytes 1572872 | tf_op jit(solution)/shard_map/ppermute | solution.py:21
  50.0 35.7 %collective-permute-start.2 = (f32[512,256]{1,0:T(8,128)S(1)}, f32[512,256]{1,0:T(8,128)S(1)}, u32[]{:S(2)}, u32[]{:S(2)}) collective-permute-start(f32[512,256]{1,0:T(8,128)S(1)} %bitcast.129), channel_id=1, source_target_pairs={{0,26},{2,28},{4,30},{6,0},{8,2},{10,4},{12,6},{14,8},{16,10},{18,... | collective-permute-start | bytes 1572872 | tf_op jit(solution)/shard_map/ppermute | solution.py:21
  73.3 23.5 %collective-permute-start.1 = (f32[512,256]{1,0:T(8,128)S(1)}, f32[512,256]{1,0:T(8,128)S(1)}, u32[]{:S(2)}, u32[]{:S(2)}) collective-permute-start(f32[512,256]{1,0:T(8,128)S(1)} %bitcast.130), channel_id=1, source_target_pairs={{0,28},{2,30},{4,0},{6,2},{8,4},{10,6},{12,8},{14,10},{16,12},{18,... | collective-permute-start | bytes 1572872 | tf_op jit(solution)/shard_map/ppermute | solution.py:21
  75.1 24.8 %collective-permute-start = (f32[512,256]{1,0:T(8,128)S(1)}, f32[512,256]{1,0:T(8,128)S(1)}, u32[]{:S(2)}, u32[]{:S(2)}) collective-permute-start(f32[512,256]{1,0:T(8,128)S(1)} %bitcast.131), channel_id=1, source_target_pairs={{0,30},{2,0},{4,2},{6,4},{8,6},{10,8},{12,10},{14,12},{16,14},{18,... | collective-permute-start | bytes 1572872 | tf_op jit(solution)/shard_map/ppermute | solution.py:21
  85.7 35.9 %collective-permute-start.5 = (f32[256,512]{1,0:T(8,128)S(1)}, f32[256,512]{1,0:T(8,128)}, u32[]{:S(2)}, u32[]{:S(2)}) collective-permute-start(f32[256,512]{1,0:T(8,128)S(1)} %copy-done.8), channel_id=1, source_target_pairs={{0,26},{2,28},{4,30},{6,0},{8,2},{10,4},{12,6},{14,8},{16,10},{18,... | collective-permute-start | bytes 1572872 | tf_op jit(solution)/shard_map/ppermute | solution.py:21
  157.2 3.4 %copy-start.1 = (f32[4,256,256]{2,1,0:T(8,128)S(1)}, f32[4,256,256]{2,1,0:T(8,128)}, u32[]{:S(2)}) copy-start(f32[4,256,256]{2,1,0:T(8,128)} %all-reduce.2.cloned.1.call-done) | copy-start | bytes 3145732
  157.2 3.4 %copy-start.2 = (f32[4,256,512]{2,1,0:T(8,128)S(1)}, f32[4,256,512]{2,1,0:T(8,128)}, u32[]{:S(2)}) copy-start(f32[4,256,512]{2,1,0:T(8,128)} %gather_fusion) | copy-start | bytes 6291460
  168.1 28.2 %copy-start.6 = (f32[256,512]{1,0:T(8,128)S(1)}, f32[256,512]{1,0:T(8,128)}, u32[]{:S(2)}) copy-start(f32[256,512]{1,0:T(8,128)} %param.16) | copy-start | bytes 1572868
  168.2 24.4 %collective-permute-start.7 = (f32[256,512]{1,0:T(8,128)S(1)}, f32[256,512]{1,0:T(8,128)S(1)}, u32[]{:S(2)}, u32[]{:S(2)}) collective-permute-start(f32[256,512]{1,0:T(8,128)S(1)} %bitcast.135), channel_id=1, source_target_pairs={{0,4},{2,6},{4,8},{6,10},{8,12},{10,14},{12,16},{14,18},{16,20},{1... | collective-permute-start | bytes 1572872 | tf_op jit(solution)/shard_map/ppermute | solution.py:21
  169.7 26.6 %collective-permute-start.8 = (f32[256,512]{1,0:T(8,128)S(1)}, f32[256,512]{1,0:T(8,128)S(1)}, u32[]{:S(2)}, u32[]{:S(2)}) collective-permute-start(f32[256,512]{1,0:T(8,128)S(1)} %bitcast.134), channel_id=1, source_target_pairs={{0,6},{2,8},{4,10},{6,12},{8,14},{10,16},{12,18},{14,20},{16,22},{... | collective-permute-start | bytes 1572872 | tf_op jit(solution)/shard_map/ppermute | solution.py:21
  171.2 25.1 %collective-permute-start.6 = (f32[256,512]{1,0:T(8,128)S(1)}, f32[256,512]{1,0:T(8,128)S(1)}, u32[]{:S(2)}, u32[]{:S(2)}) collective-permute-start(f32[256,512]{1,0:T(8,128)S(1)} %bitcast.133), channel_id=1, source_target_pairs={{0,2},{2,4},{4,6},{6,8},{8,10},{10,12},{12,14},{14,16},{16,18},{18... | collective-permute-start | bytes 1572872 | tf_op jit(solution)/shard_map/ppermute | solution.py:21
  196.7 36.9 %copy-start.4 = (f32[256,512]{1,0:T(8,128)}, f32[256,512]{1,0:T(8,128)S(1)}, u32[]{:S(2)}) copy-start(f32[256,512]{1,0:T(8,128)S(1)} %fusion.45) | copy-start | bytes 1572868
  196.7 24.7 %collective-permute-start.11 = (f32[256,512]{1,0:T(8,128)S(1)}, f32[256,512]{1,0:T(8,128)S(1)}, u32[]{:S(2)}, u32[]{:S(2)}) collective-permute-start(f32[256,512]{1,0:T(8,128)S(1)} %fusion.45), channel_id=1, source_target_pairs={{0,26},{2,28},{4,30},{6,0},{8,2},{10,4},{12,6},{14,8},{16,10},{18,... | collective-permute-start | bytes 1572872 | tf_op jit(solution)/shard_map/ppermute | solution.py:21
  200.3 33.0 %collective-permute-start.10 = (f32[256,512]{1,0:T(8,128)S(1)}, f32[256,512]{1,0:T(8,128)S(1)}, u32[]{:S(2)}, u32[]{:S(2)}) collective-permute-start(f32[256,512]{1,0:T(8,128)S(1)} %fusion.45), channel_id=1, source_target_pairs={{0,28},{2,30},{4,0},{6,2},{8,4},{10,6},{12,8},{14,10},{16,12},{18,... | collective-permute-start | bytes 1572872 | tf_op jit(solution)/shard_map/ppermute | solution.py:21
  211.8 21.5 %collective-permute-start.9 = (f32[256,512]{1,0:T(8,128)S(1)}, f32[256,512]{1,0:T(8,128)S(1)}, u32[]{:S(2)}, u32[]{:S(2)}) collective-permute-start(f32[256,512]{1,0:T(8,128)S(1)} %fusion.45), channel_id=1, source_target_pairs={{0,30},{2,0},{4,2},{6,4},{8,6},{10,8},{12,10},{14,12},{16,14},{18,... | collective-permute-start | bytes 1572872 | tf_op jit(solution)/shard_map/ppermute | solution.py:21
  241.5 3.4 %copy-start.3 = (f32[4,256,512]{2,1,0:T(8,128)S(1)}, f32[4,256,512]{2,1,0:T(8,128)}, u32[]{:S(2)}) copy-start(f32[4,256,512]{2,1,0:T(8,128)} %gather_fusion.2) | copy-start | bytes 6291460
  251.5 47.8 %copy-start.5 = (f32[256,512]{1,0:T(8,128)S(1)}, f32[256,512]{1,0:T(8,128)}, u32[]{:S(2)}) copy-start(f32[256,512]{1,0:T(8,128)} %copy-done.4) | copy-start | bytes 1572868
  251.5 47.8 %copy-start.7 = (f32[256,512]{1,0:T(8,128)S(1)}, f32[256,512]{1,0:T(8,128)}, u32[]{:S(2)}) copy-start(f32[256,512]{1,0:T(8,128)} %param.16) | copy-start | bytes 1572868
  251.6 22.4 %collective-permute-start.12 = (f32[256,512]{1,0:T(8,128)S(1)}, f32[256,512]{1,0:T(8,128)S(1)}, u32[]{:S(2)}, u32[]{:S(2)}) collective-permute-start(f32[256,512]{1,0:T(8,128)S(1)} %get-tuple-element.43), channel_id=1, source_target_pairs={{0,2},{2,4},{4,6},{6,8},{8,10},{10,12},{12,14},{14,16},{16,18},{18... | collective-permute-start | bytes 1572872 | tf_op jit(solution)/shard_map/ppermute | solution.py:21
  253.2 27.0 %collective-permute-start.14 = (f32[256,512]{1,0:T(8,128)S(1)}, f32[256,512]{1,0:T(8,128)S(1)}, u32[]{:S(2)}, u32[]{:S(2)}) collective-permute-start(f32[256,512]{1,0:T(8,128)S(1)} %get-tuple-element.44), channel_id=1, source_target_pairs={{0,6},{2,8},{4,10},{6,12},{8,14},{10,16},{12,18},{14,20},{16,22},{... | collective-permute-start | bytes 1572872 | tf_op jit(solution)/shard_map/ppermute | solution.py:21
  260.5 38.8 %collective-permute-start.13 = (f32[256,512]{1,0:T(8,128)S(1)}, f32[256,512]{1,0:T(8,128)S(1)}, u32[]{:S(2)}, u32[]{:S(2)}) collective-permute-start(f32[256,512]{1,0:T(8,128)S(1)} %get-tuple-element.45), channel_id=1, source_target_pairs={{0,4},{2,6},{4,8},{6,10},{8,12},{10,14},{12,16},{14,18},{16,20},{1... | collective-permute-start | bytes 1572872 | tf_op jit(solution)/shard_map/ppermute | solution.py:21
Sparse Core Ops, SparseCore 0:
  117.1 35.9 all-reduce.1
